TPU v7x, 32 devices: a whole 2x2x4 slice. The times are simulated.
32 devices in a mesh: parts: 2 (over y), row: 4 (over z), col: 2 (over x), rhs: 2 (over core).
Axes of the slice: x: 2, y: 2, z: 4, core: 2. Of those that a mesh axis runs over, the one named last changes fastest.
Arguments:
- blocks: bfloat16 [8, 2, 96, 128, 128], P(('parts', 'row'), 'col'), parts along dimension 0, as said below
- block_rows: int32 [8, 2, 96], P(('parts', 'row'), 'col'), parts along dimension 0, may hold values from 0 to 127, as said below
- block_cols: int32 [8, 2, 96], P(('parts', 'row'), 'col'), parts along dimension 0, may hold values from 0 to 255, as said below
- counts: int32 [8, 2], P(('parts', 'row'), 'col'), parts along dimension 0, may hold values from 1 to 96, as said below
- diagonal: float32 [131072], P(('parts', 'row', 'col')), parts along dimension 0, may hold values from 1.2 to 4
- target: float32 [131072, 256], P(('parts', 'row', 'col'), 'rhs'), parts along dimension 0, may hold values from -6 to 6
Outputs:
- solution: float32 [131072, 256], P(('parts', 'row', 'col'), 'rhs'), parts along dimension 0
- residual: float32 [131072, 256], P(('parts', 'row', 'col'), 'rhs'), parts along dimension 0
There are 2 independent parts, one for each index of `parts`. A program takes and returns all parts, laid end to end along the dimension named above; each array names one. Nothing has to cross between parts.
Inputs may be any that keep to these rules, and one draw needn't show every extreme that they name: Each tile's used slots are its first counts slots; the busiest tile has exactly 96. `block_rows`: used slots of one tile name distinct blocks on or above the diagonal. `block_cols`: see block_rows. `blocks`: unused slots hold values that do not enter the operator; the operator is positive definite.
All inputs are finite; a program needn't handle non-finite values.
Results may differ from a plain program's by a relative error of at most 0.0045.
Values may be sent and summed in bfloat16 or wider, within the bound.
A program may use at most 128 MiB of HBM per device.

v0:
```python
import jax
import jax.numpy as jnp
from jax import lax
from jax.sharding import PartitionSpec as P

ITERS = 2


def one_hot_slots(indices, valid, extent):
    return ((indices[None, :] == jnp.arange(extent)[:, None]) & valid[None, :]).astype(jnp.float32)


def on_device(blocks, block_rows, block_cols, counts, diagonal, target):
    highest = lax.Precision.HIGHEST
    nrow = lax.axis_size("row")
    ncol = lax.axis_size("col")
    stored = blocks[0, 0]
    slots = stored.shape[0]
    width = stored.shape[1]
    local = target.shape[0]
    ncols = target.shape[1]
    quarter = local // width
    row_blocks = ncol * quarter
    col_blocks = nrow * quarter
    valid = jnp.arange(slots) < counts[0, 0]
    rows_hot = one_hot_slots(block_rows[0, 0], valid, row_blocks)
    cols_hot = one_hot_slots(block_cols[0, 0], valid, col_blocks)

    def squares(vector):
        return lax.psum(jnp.sum(vector * vector, axis=0), ("row", "col"))

    solution = jnp.zeros_like(target)
    residual = target
    direction = target
    norm_now = squares(residual)
    for step in range(ITERS):
        operate_field_low = direction.astype(jnp.bfloat16)
        direct_gathered = lax.all_gather(operate_field_low, "row", axis=0, tiled=True).reshape(
            col_blocks, width, ncols
        )
        prod = jnp.einsum(
            "kab,kbc->kac",
            stored,
            direct_gathered[block_cols[0, 0]],
            preferred_element_type=jnp.float32,
        )
        direct_partial_value = jnp.einsum("ik,kac->iac", rows_hot, prod, precision=highest)
        direct = lax.psum_scatter(
            direct_partial_value.reshape(row_blocks * width, ncols).astype(jnp.bfloat16),
            "col",
            scatter_dimension=0,
            tiled=True,
        ).astype(jnp.float32)
        gathered = lax.all_gather(operate_field_low, "col", axis=0, tiled=True).reshape(
            row_blocks, width, ncols
        )
        tprod = jnp.einsum(
            "kba,kbc->kac", stored, gathered[block_rows[0, 0]], preferred_element_type=jnp.float32
        )
        partial_value = jnp.einsum("jk,kac->jac", cols_hot, tprod, precision=highest)
        parcel = partial_value.astype(jnp.bfloat16).reshape(nrow, local, ncols)
        mirrored = jnp.sum(
            lax.all_to_all(parcel, "row", split_axis=0, concat_axis=0, tiled=True).astype(
                jnp.float32
            ),
            axis=0,
        )
        image = diagonal[:, None] * direction + direct + mirrored
        curve = lax.psum(jnp.sum(direction * image, axis=0), ("row", "col"))
        alpha = norm_now / curve
        solution = solution + alpha * direction
        residual = residual - alpha * image
        if step + 1 < ITERS:
            norm_next = squares(residual)
            direction = residual + norm_next / norm_now * direction
            norm_now = norm_next
    return (solution, residual)


def solution(mesh):
    return jax.shard_map(
        on_device,
        mesh=mesh,
        in_specs=(
            P(("parts", "row"), "col", None, None, None),
            P(("parts", "row"), "col", None),
            P(("parts", "row"), "col", None),
            P(("parts", "row"), "col"),
            P(("parts", "row", "col")),
            P(("parts", "row", "col"), "rhs"),
        ),
        out_specs=(P(("parts", "row", "col"), "rhs"), P(("parts", "row", "col"), "rhs")),
        check_vma=False,
    )
```

profile of v0, /device:TPU:0, one launch (start us, length us, event | category | flops | bytes accessed | tf_op | source)
XLA Modules:
  0.0 973.1 jit_solution(810773173325068209)
XLA Ops:
  12.6 58.2 %all-gather.7.cloned.1.call-done = bf16[16384,128]{1,0:T(8,128)(2,1)} async-done(((bf16[8192,128]{1,0:T(8,128)(2,1)}), bf16[16384,128]{1,0:T(8,128)(2,1)}) %all-gather.7.cloned.1.call-update) | async-done | bytes 4194320 | tf_op jit(solution)/shard_map/all_gather | solution.py:54
  75.6 6.2 fusion.10
  81.8 7.1 copy.13
  88.9 13.1 %convolution_convert_fusion.1 = bf16[256,128,128]{2,0,1:T(8,128)(2,1)} fusion(f32[96,128,128]{1,0,2:T(8,128)} %copy.13, s32[96]{0:T(128)S(1)} %bitcast.65, pred[96]{0:T(512)(128)(4,1)S(1)} %iota_compare_fusion.2), kind=kOutput, calls=%fused_computation.7 | convolution fusion | flops 4836081664 | bytes 14680544 | tf_op jit(solution)/shard_map/jk,kac->jac/dot_general | solution.py:60
  102.0 12.0 %copy.9 = bf16[256,128,128]{2,1,0:T(8,128)(2,1)} copy(bf16[256,128,128]{2,0,1:T(8,128)(2,1)} %convolution_convert_fusion.1) | data formatting | bytes 16777216 | tf_op jit(solution)/shard_map/convert_element_type | solution.py:61
  120.2 242.3 %all-gather.5.cloned.1.call-done = bf16[32768,128]{1,0:T(8,128)(2,1)} async-done(((bf16[8192,128]{1,0:T(8,128)(2,1)}), bf16[32768,128]{1,0:T(8,128)(2,1)}) %all-gather.5.cloned.1.call-update) | async-done | bytes 8388624 | tf_op jit(solution)/shard_map/all_gather | solution.py:38
  362.6 6.1 gather_fusion
  368.6 6.9 fusion.12
  375.5 6.6 copy.12
  382.2 7.1 fusion.14
  394.0 7.7 all-to-all-done
  401.7 7.0 convert_reduce_fusion.1
  408.7 37.9 %reduce-scatter.3.cloned.1.call-done = bf16[8192,128]{1,0:T(8,128)(2,1)} async-done(((bf16[16384,128]{1,0:T(8,128)(2,1)}), bf16[8192,128]{1,0:T(8,128)(2,1)}) %reduce-scatter.3.cloned.1.call-update) | async-done | bytes 2097168 | tf_op jit(solution)/shard_map/reduce_scatter | solution.py:48
  451.2 20.4 %all-reduce = (f32[128]{0:T(128)S(1)}, f32[128]{0:T(128)S(1)}) all-reduce(f32[128]{0:T(128)S(1)} %get-tuple-element.3, f32[128]{0:T(128)S(1)} %get-tuple-element.2), channel_id=1, replica_groups=mesh['parts'=2,'row'=4,'col'=2,'rhs'=2] {'row','col'}, use_global_device_ids=true, to_apply=%region_1.0 | all-reduce | flops 256 | bytes 2048 | tf_op jit(solution)/shard_map/psum | solution.py:30
  471.6 5.9 multiply_reduce_fusion.1
  477.6 17.1 %psum.30 = f32[128]{0:T(128)S(1)} all-reduce(f32[128]{0:T(128)S(1)} %get-tuple-element.6), channel_id=1, replica_groups=mesh['parts'=2,'row'=4,'col'=2,'rhs'=2] {'row','col'}, use_global_device_ids=true, to_apply=%region_7.0 | all-reduce | flops 128 | bytes 1024 | tf_op jit(solution)/shard_map/psum | solution.py:30
  500.6 55.0 %all-gather.11.cloned.1.call-done = bf16[16384,128]{1,0:T(8,128)(2,1)} async-done(((bf16[8192,128]{1,0:T(8,128)(2,1)}), bf16[16384,128]{1,0:T(8,128)(2,1)}) %all-gather.11.cloned.1.call-update) | async-done | bytes 4194320 | tf_op jit(solution)/shard_map/all_gather | solution.py:54
  560.5 6.1 fusion.6
  566.6 7.0 copy.15
  573.6 13.1 %convolution_convert_fusion = bf16[256,128,128]{2,0,1:T(8,128)(2,1)} fusion(f32[96,128,128]{1,0,2:T(8,128)} %copy.15, s32[96]{0:T(128)S(1)} %bitcast.66, pred[96]{0:T(512)(128)(4,1)S(1)} %iota_compare_fusion.2), kind=kOutput, calls=%fused_computation.6 | convolution fusion | flops 4836081664 | bytes 14680544 | tf_op jit(solution)/shard_map/jk,kac->jac/dot_general | solution.py:60
  586.7 12.1 %copy.11 = bf16[256,128,128]{2,1,0:T(8,128)(2,1)} copy(bf16[256,128,128]{2,0,1:T(8,128)(2,1)} %convolution_convert_fusion) | data formatting | bytes 16777216 | tf_op jit(solution)/shard_map/convert_element_type | solution.py:61
  604.5 242.3 %all-gather.9.cloned.1.call-done = bf16[32768,128]{1,0:T(8,128)(2,1)} async-done(((bf16[8192,128]{1,0:T(8,128)(2,1)}), bf16[32768,128]{1,0:T(8,128)(2,1)}) %all-gather.9.cloned.1.call-update) | async-done | bytes 8388624 | tf_op jit(solution)/shard_map/all_gather | solution.py:38
  846.8 6.1 gather_fusion.2
  852.9 6.9 fusion.8
  859.8 6.8 copy.14
  866.6 7.1 fusion.17
  878.3 7.6 all-to-all-done.1
  885.9 7.0 convert_reduce_fusion
  893.0 37.9 %reduce-scatter.5.cloned.1.call-done = bf16[8192,128]{1,0:T(8,128)(2,1)} async-done(((bf16[16384,128]{1,0:T(8,128)(2,1)}), bf16[8192,128]{1,0:T(8,128)(2,1)}) %reduce-scatter.5.cloned.1.call-update) | async-done | bytes 2097168 | tf_op jit(solution)/shard_map/reduce_scatter | solution.py:48
  930.9 5.9 multiply_reduce_fusion
  936.8 20.4 %psum.31 = f32[128]{0:T(128)S(1)} all-reduce(f32[128]{0:T(128)S(1)} %multiply_reduce_fusion), channel_id=1, replica_groups=mesh['parts'=2,'row'=4,'col'=2,'rhs'=2] {'row','col'}, use_global_device_ids=true, to_apply=%region_11.0 | all-reduce | flops 128 | bytes 1024 | tf_op jit(solution)/shard_map/psum | solution.py:69
  957.2 8.7 multiply_subtract_fusion
  (37 shorter events, 46.3 us)
Async XLA Ops:
  7.2 68.5 %copy-start = (bf16[1,1,96,128,128]{4,3,2,1,0:T(8,128)(2,1)S(1)}, bf16[1,1,96,128,128]{4,3,2,1,0:T(8,128)(2,1)}, u32[]{:S(2)}) copy-start(bf16[1,1,96,128,128]{4,3,2,1,0:T(8,128)(2,1)} %param.6) | copy-start | bytes 9437188
  7.2 5.4 copy-start.3
  7.2 63.5 %all-gather.7.cloned.1.call-start = ((), (), s32[]{:S(2)}) async-start(), calls=%async_computation.6 | async-start | bytes 6291456 | tf_op jit(solution)/shard_map/all_gather | solution.py:54
  11.1 351.4 %all-gather.5.cloned.1.call-start = ((), (), s32[]{:S(2)}) async-start(), calls=%async_computation.4 | async-start | bytes 10485760 | tf_op jit(solution)/shard_map/all_gather | solution.py:38
  81.8 7.1 copy-start.2
  114.1 287.7 %all-to-all-start = ((bf16[4,8192,128]{2,1,0:T(8,128)(2,1)}), bf16[4,8192,128]{2,1,0:T(8,128)(2,1)}, u32[]{:S(2)}, u32[]{:S(2)}) async-start(bf16[4,8192,128]{2,1,0:T(8,128)(2,1)} %bitcast.57), calls=%async_computation.1 | async-start | bytes 16777216 | tf_op jit(solution)/shard_map/all_to_all | solution.py:63
  119.7 326.8 %reduce-scatter.3.cloned.1.call-start = ((), (), s32[]{:S(2)}) async-start(), calls=%async_computation.5 | async-start | bytes 6291456 | tf_op jit(solution)/shard_map/reduce_scatter | solution.py:48
  394.0 52.6 %copy-start.1 = (f32[8192]{0:T(1024)S(1)}, f32[8192]{0:T(1024)}, u32[]{:S(2)}) copy-start(f32[8192]{0:T(1024)} %param.10) | copy-start | bytes 98308
  394.0 161.6 %all-gather.11.cloned.1.call-start = ((), (), s32[]{:S(2)}) async-start(), calls=%async_computation.9 | async-start | bytes 6291456 | tf_op jit(solution)/shard_map/all_gather | solution.py:54
  500.0 346.8 %all-gather.9.cloned.1.call-start = ((), (), s32[]{:S(2)}) async-start(), calls=%async_computation.7 | async-start | bytes 10485760 | tf_op jit(solution)/shard_map/all_gather | solution.py:38
  598.8 287.1 %all-to-all-start.1 = ((bf16[4,8192,128]{2,1,0:T(8,128)(2,1)}), bf16[4,8192,128]{2,1,0:T(8,128)(2,1)}, u32[]{:S(2)}, u32[]{:S(2)}) async-start(bf16[4,8192,128]{2,1,0:T(8,128)(2,1)} %bitcast.58), calls=%async_computation.3 | async-start | bytes 16777216 | tf_op jit(solution)/shard_map/all_to_all | solution.py:63
  604.5 326.4 %reduce-scatter.5.cloned.1.call-start = ((), (), s32[]{:S(2)}) async-start(), calls=%async_computation.8 | async-start | bytes 6291456 | tf_op jit(solution)/shard_map/reduce_scatter | solution.py:48
Sparse Core Ops, SparseCore 0:
  11.2 59.4 all-gather.6
  72.9 289.6 all-gather.4
  394.1 52.4 reduce-scatter.2
  500.1 55.4 all-gather.10
  557.1 289.6 all-gather.8
  878.4 52.4 reduce-scatter.4
where the time goes:
time: 976 us; the launch traced here: 973 us
  waiting for transfers between devices  690 us (71%)
  local copies, waits for them, and re-layouts  83 us (9%)
  matrix products  66.4 us (7%)
  blocking collectives  58 us (6%)
  other arithmetic  48.4 us (5%)
  between operations  15.1 us (2%)
  starting transfers between devices  12 us (1%)
    all_gather x2, waiting for transfers between devices, on_device(): lax.all_gather(operate_field_low, 'row', axis=0, tiled=True)  485 us
    all_gather x2, waiting for transfers between devices, on_device(): lax.all_gather(operate_field_low, 'col', axis=0, tiled=True)  113 us
    reduce_scatter x2, waiting for transfers between devices, on_device(): lax.psum_scatter(direct_partial_value.reshape(row_blocks * width, ncols)....  75.8 us
    psum x2, blocking collectives, squares(): return lax.psum(jnp.sum(vector * vector, axis=0), ('row', 'col'))  37.6 us
    dot_general x2, matrix products, on_device(): jnp.einsum('jk,kac->jac', cols_hot, tprod, precision=highest)  26.2 us
    convert_element_type x2, local copies, waits for them, and re-layouts, on_device(): parcel = partial_value.astype(jnp.bfloat16).reshape(nrow, local, ncols)  24.1 us
    psum x1, blocking collectives, on_device(): curve = lax.psum(jnp.sum(direction * image, axis=0), ('row', 'col'))  20.4 us
  transfers between devices with their start and end apart: 8, of which 8 were waited for; matrix products, arithmetic and copies ran while one was open for 17% of the time, Pallas kernels for 0%

commit v1 on v0

--- a/solution.py
+++ b/solution.py
@@ -66,7 +66,7 @@
             axis=0,
         )
         image = diagonal[:, None] * direction + direct + mirrored
-        curve = lax.psum(jnp.sum(direction * image, axis=0), ("row", "col"))
+        curve = lax.psum(lax.psum(jnp.sum(direction * image, axis=0), "col"), "row")
         alpha = norm_now / curve
         solution = solution + alpha * direction
         residual = residual - alpha * image

time: 976 us -> 986 us (1.010)
  blocking collectives: 58 us -> 68.8 us
    psum x1 -> x4, blocking collectives: 20.4 us -> 29.9 us  [on_device(): curve = lax.psum(lax.psum(jnp.sum(direction * image, axis=0), 'col'), 'row')]
where the time goes in v1:
time: 986 us; the launch traced here: 982 us
  waiting for transfers between devices  689 us (70%)
  local copies, waits for them, and re-layouts  83 us (8%)
  blocking collectives  68.8 us (7%)
  matrix products  66.4 us (7%)
  other arithmetic  48.4 us (5%)
  between operations  15.1 us (2%)
  starting transfers between devices  12 us (1%)
    all_gather x2, waiting for transfers between devices, on_device(): lax.all_gather(operate_field_low, 'row', axis=0, tiled=True)  485 us
    all_gather x2, waiting for transfers between devices, on_device(): lax.all_gather(operate_field_low, 'col', axis=0, tiled=True)  112 us
    reduce_scatter x2, waiting for transfers between devices, on_device(): lax.psum_scatter(direct_partial_value.reshape(row_blocks * width, ncols)....  75.8 us
    psum x2, blocking collectives, squares(): return lax.psum(jnp.sum(vector * vector, axis=0), ('row', 'col'))  39 us
    psum x4, blocking collectives, on_device(): curve = lax.psum(lax.psum(jnp.sum(direction * image, axis=0), 'col'), 'row')  29.9 us
    dot_general x2, matrix products, on_device(): jnp.einsum('jk,kac->jac', cols_hot, tprod, precision=highest)  26.2 us
    convert_element_type x2, local copies, waits for them, and re-layouts, on_device(): parcel = partial_value.astype(jnp.bfloat16).reshape(nrow, local, ncols)  24.1 us
  transfers between devices with their start and end apart: 8, of which 8 were waited for; matrix products, arithmetic and copies ran while one was open for 17% of the time, Pallas kernels for 0%

profile of v1, /device:TPU:0, one launch (start us, length us, event | category | flops | bytes accessed | tf_op | source)
XLA Modules:
  0.0 982.5 jit_solution(16324997306976758205)
XLA Ops:
  12.6 58.2 %all-gather.7.cloned.1.call-done = bf16[16384,128]{1,0:T(8,128)(2,1)} async-done(((bf16[8192,128]{1,0:T(8,128)(2,1)}), bf16[16384,128]{1,0:T(8,128)(2,1)}) %all-gather.7.cloned.1.call-update) | async-done | bytes 4194320 | tf_op jit(solution)/shard_map/all_gather | solution.py:54
  75.6 6.2 fusion.10
  81.8 7.1 copy.13
  88.9 13.1 %convolution_convert_fusion.1 = bf16[256,128,128]{2,0,1:T(8,128)(2,1)} fusion(f32[96,128,128]{1,0,2:T(8,128)} %copy.13, s32[96]{0:T(128)S(1)} %bitcast.65, pred[96]{0:T(512)(128)(4,1)S(1)} %iota_compare_fusion.2), kind=kOutput, calls=%fused_computation.7 | convolution fusion | flops 4836081664 | bytes 14680544 | tf_op jit(solution)/shard_map/jk,kac->jac/dot_general | solution.py:60
  102.0 12.0 %copy.9 = bf16[256,128,128]{2,1,0:T(8,128)(2,1)} copy(bf16[256,128,128]{2,0,1:T(8,128)(2,1)} %convolution_convert_fusion.1) | data formatting | bytes 16777216 | tf_op jit(solution)/shard_map/convert_element_type | solution.py:61
  120.2 242.3 %all-gather.5.cloned.1.call-done = bf16[32768,128]{1,0:T(8,128)(2,1)} async-done(((bf16[8192,128]{1,0:T(8,128)(2,1)}), bf16[32768,128]{1,0:T(8,128)(2,1)}) %all-gather.5.cloned.1.call-update) | async-done | bytes 8388624 | tf_op jit(solution)/shard_map/all_gather | solution.py:38
  362.6 6.1 gather_fusion
  368.6 6.9 fusion.12
  375.5 6.6 copy.12
  382.2 7.1 fusion.14
  394.0 7.7 all-to-all-done
  401.7 7.0 convert_reduce_fusion.1
  408.7 37.9 %reduce-scatter.3.cloned.1.call-done = bf16[8192,128]{1,0:T(8,128)(2,1)} async-done(((bf16[16384,128]{1,0:T(8,128)(2,1)}), bf16[8192,128]{1,0:T(8,128)(2,1)}) %reduce-scatter.3.cloned.1.call-update) | async-done | bytes 2097168 | tf_op jit(solution)/shard_map/reduce_scatter | solution.py:48
  451.2 20.4 %psum.42 = f32[128]{0:T(128)S(1)} all-reduce(f32[128]{0:T(128)S(1)} %get-tuple-element.3), channel_id=1, replica_groups=mesh['parts'=2,'row'=4,'col'=2,'rhs'=2] {'row','col'}, use_global_device_ids=true, to_apply=%region_1.0 | all-reduce | flops 128 | bytes 1024 | tf_op jit(solution)/shard_map/psum | solution.py:30
  476.6 8.3 psum.44
  484.9 5.9 multiply_reduce_fusion.1
  490.8 18.5 %psum.45 = f32[128]{0:T(128)S(1)} all-reduce(f32[128]{0:T(128)S(1)} %get-tuple-element.4), channel_id=1, replica_groups=mesh['parts'=2,'row'=4,'col'=2,'rhs'=2] {'row','col'}, use_global_device_ids=true, to_apply=%region_8.0 | all-reduce | flops 128 | bytes 1024 | tf_op jit(solution)/shard_map/psum | solution.py:30
  515.3 53.6 %all-gather.11.cloned.1.call-done = bf16[16384,128]{1,0:T(8,128)(2,1)} async-done(((bf16[8192,128]{1,0:T(8,128)(2,1)}), bf16[16384,128]{1,0:T(8,128)(2,1)}) %all-gather.11.cloned.1.call-update) | async-done | bytes 4194320 | tf_op jit(solution)/shard_map/all_gather | solution.py:54
  573.8 6.1 fusion.6
  579.9 7.0 copy.15
  586.9 13.1 %convolution_convert_fusion = bf16[256,128,128]{2,0,1:T(8,128)(2,1)} fusion(f32[96,128,128]{1,0,2:T(8,128)} %copy.15, s32[96]{0:T(128)S(1)} %bitcast.66, pred[96]{0:T(512)(128)(4,1)S(1)} %iota_compare_fusion.2), kind=kOutput, calls=%fused_computation.6 | convolution fusion | flops 4836081664 | bytes 14680544 | tf_op jit(solution)/shard_map/jk,kac->jac/dot_general | solution.py:60
  600.0 12.1 %copy.11 = bf16[256,128,128]{2,1,0:T(8,128)(2,1)} copy(bf16[256,128,128]{2,0,1:T(8,128)(2,1)} %convolution_convert_fusion) | data formatting | bytes 16777216 | tf_op jit(solution)/shard_map/convert_element_type | solution.py:61
  617.8 242.3 %all-gather.9.cloned.1.call-done = bf16[32768,128]{1,0:T(8,128)(2,1)} async-done(((bf16[8192,128]{1,0:T(8,128)(2,1)}), bf16[32768,128]{1,0:T(8,128)(2,1)}) %all-gather.9.cloned.1.call-update) | async-done | bytes 8388624 | tf_op jit(solution)/shard_map/all_gather | solution.py:38
  860.0 6.1 gather_fusion.2
  866.1 6.9 fusion.8
  873.0 6.8 copy.14
  879.9 7.1 fusion.17
  891.6 7.6 all-to-all-done.1
  899.2 7.0 convert_reduce_fusion
  906.2 37.9 %reduce-scatter.5.cloned.1.call-done = bf16[8192,128]{1,0:T(8,128)(2,1)} async-done(((bf16[16384,128]{1,0:T(8,128)(2,1)}), bf16[8192,128]{1,0:T(8,128)(2,1)}) %reduce-scatter.5.cloned.1.call-update) | async-done | bytes 2097168 | tf_op jit(solution)/shard_map/reduce_scatter | solution.py:48
  955.0 11.7 %psum.47 = f32[128]{0:T(128)S(1)} all-reduce(f32[128]{0:T(128)S(1)} %psum.46), channel_id=1, replica_groups=mesh['parts'=2,'row'=4,'col'=2,'rhs'=2] {'row'}, use_global_device_ids=true, to_apply=%region_13.0 | all-reduce | flops 128 | bytes 1024 | tf_op jit(solution)/shard_map/psum | solution.py:69
  966.7 8.7 multiply_subtract_fusion
  (40 shorter events, 62.0 us)
Async XLA Ops:
  7.2 68.5 %copy-start = (bf16[1,1,96,128,128]{4,3,2,1,0:T(8,128)(2,1)S(1)}, bf16[1,1,96,128,128]{4,3,2,1,0:T(8,128)(2,1)}, u32[]{:S(2)}) copy-start(bf16[1,1,96,128,128]{4,3,2,1,0:T(8,128)(2,1)} %param.6) | copy-start | bytes 9437188
  7.2 5.4 copy-start.3
  7.2 63.5 %all-gather.7.cloned.1.call-start = ((), (), s32[]{:S(2)}) async-start(), calls=%async_computation.6 | async-start | bytes 6291456 | tf_op jit(solution)/shard_map/all_gather | solution.py:54
  11.1 351.4 %all-gather.5.cloned.1.call-start = ((), (), s32[]{:S(2)}) async-start(), calls=%async_computation.4 | async-start | bytes 10485760 | tf_op jit(solution)/shard_map/all_gather | solution.py:38
  81.8 7.1 copy-start.2
  114.1 287.7 %all-to-all-start = ((bf16[4,8192,128]{2,1,0:T(8,128)(2,1)}), bf16[4,8192,128]{2,1,0:T(8,128)(2,1)}, u32[]{:S(2)}, u32[]{:S(2)}) async-start(bf16[4,8192,128]{2,1,0:T(8,128)(2,1)} %bitcast.57), calls=%async_computation.1 | async-start | bytes 16777216 | tf_op jit(solution)/shard_map/all_to_all | solution.py:63
  119.7 326.8 %reduce-scatter.3.cloned.1.call-start = ((), (), s32[]{:S(2)}) async-start(), calls=%async_computation.5 | async-start | bytes 6291456 | tf_op jit(solution)/shard_map/reduce_scatter | solution.py:48
  394.0 52.6 %copy-start.1 = (f32[8192]{0:T(1024)S(1)}, f32[8192]{0:T(1024)}, u32[]{:S(2)}) copy-start(f32[8192]{0:T(1024)} %param.10) | copy-start | bytes 98308
  394.0 174.9 %all-gather.11.cloned.1.call-start = ((), (), s32[]{:S(2)}) async-start(), calls=%async_computation.9 | async-start | bytes 6291456 | tf_op jit(solution)/shard_map/all_gather | solution.py:54
  514.7 345.3 %all-gather.9.cloned.1.call-start = ((), (), s32[]{:S(2)}) async-start(), calls=%async_computation.7 | async-start | bytes 10485760 | tf_op jit(solution)/shard_map/all_gather | solution.py:38
  612.1 287.1 %all-to-all-start.1 = ((bf16[4,8192,128]{2,1,0:T(8,128)(2,1)}), bf16[4,8192,128]{2,1,0:T(8,128)(2,1)}, u32[]{:S(2)}, u32[]{:S(2)}) async-start(bf16[4,8192,128]{2,1,0:T(8,128)(2,1)} %bitcast.58), calls=%async_computation.3 | async-start | bytes 16777216 | tf_op jit(solution)/shard_map/all_to_all | solution.py:63
  617.7 326.4 %reduce-scatter.5.cloned.1.call-start = ((), (), s32[]{:S(2)}) async-start(), calls=%async_computation.8 | async-start | bytes 6291456 | tf_op jit(solution)/shard_map/reduce_scatter | solution.py:48
Sparse Core Ops, SparseCore 0:
  11.2 59.4 all-gather.6
  72.9 289.6 all-gather.4
  394.1 52.4 reduce-scatter.2
  514.8 53.9 all-gather.10
  570.4 289.6 all-gather.8
  891.7 52.4 reduce-scatter.4
